TPU v7x, 512 devices: a whole 4x4x16 slice. The times are simulated.
512 devices in a mesh: stn: 64 (over x, y, z_hi, core), chan: 8 (over z_lo).
Axes of the slice: x: 4, y: 4, z: 16 (z_hi: 2, z_lo: 8; z = z_hi * 8 + z_lo), core: 2. Of those that a mesh axis runs over, the one named last changes fastest.
Arguments:
- voltages: bfloat16 [512, 2, 2, 8, 4864], P('stn', None, None, 'chan'), may hold values from -6 to 6
- prototype: float32 [16, 256], replicated, may hold values from -1.5 to 1.5
- kernel_table: float32 [8, 7], replicated, may hold values from 0.05 to 1
- tile_subgrid: int32 [8, 512, 4, 512, 1], P('chan', 'stn'), may hold values from 0 to 31; in each aligned block of 16384 rows (0 to 16383, 16384 to 32767, ..., all dimensions but the last counted through in order) at most 1024 rows name the same one
- tile_cells: int32 [8, 512, 4, 512, 2], P('chan', 'stn'), may hold values from 3 to 44
- tile_offsets: int32 [8, 512, 4, 512, 2], P('chan', 'stn'), may hold values from 0 to 7
- subgrid_slot: int32 [32], replicated, may hold values from 0 to 31, each once
Outputs:
- uv_grid: float32 [32, 48, 384], P('chan', None, 'stn')
Inputs may be any that keep to these rules, and one draw needn't show every extreme that they name: `tile_subgrid`: among the tiles of one device (one coarse channel c and the 8 stations a of one index of stn), no subgrid is named more than 1024 times, and in every draw some device's tiles name some subgrid exactly 1024 times. `subgrid_slot`: each of 0 to 31 appears once.
All inputs are finite; a program needn't handle non-finite values.
Results may differ from a plain program's by a relative error of at most 0.0066.
Values may be sent and summed in bfloat16 or wider, within the bound.
No kernel may reach another device: no remote copies, remote signals or barrier semaphores. Data moves between devices by JAX's collectives and lax.ppermute only.
A program may use at most 128 MiB of HBM per device.

v0:
```python
import math

import jax
import jax.numpy as jnp
from jax import lax
from jax.sharding import PartitionSpec as P

FINE = 256
TAPS = 16
FRAMES = 4
CT = 4
G = 48
NSUB = 32
KW = 7


def fourier_table(length):
    index = jnp.arange(length, dtype=jnp.int32)
    phase = index[:, None] * index[None, :] % length
    angle = phase.astype(jnp.float32) * (2.0 * math.pi / length)
    cosine = jnp.cos(angle) / math.sqrt(length)
    sine = jnp.sin(angle) / math.sqrt(length)
    upper = jnp.concatenate([cosine, -sine], axis=1)
    lower = jnp.concatenate([sine, cosine], axis=1)
    return jnp.concatenate([upper, lower], axis=0)


def channelize(voltages, prototype):
    stations = voltages.shape[0]
    samples = (
        voltages[:, :, :, 0, :].astype(jnp.float32).reshape(stations, 2, 2, FRAMES + TAPS - 1, FINE)
    )
    filtered = jnp.zeros((stations, 2, 2, FRAMES, FINE), jnp.float32)
    for tap in range(TAPS):
        filtered = filtered + prototype[tap] * samples[:, :, :, tap : tap + FRAMES, :]
    frame_rows = filtered.transpose(0, 1, 3, 2, 4).reshape(stations * 2 * FRAMES, 2 * FINE)
    spectra = jnp.dot(frame_rows, fourier_table(FINE), precision=lax.Precision.HIGHEST).astype(
        jnp.bfloat16
    )
    spectra = spectra.reshape(stations, 2, FRAMES, 2, CT, FINE // CT)
    return spectra.transpose(4, 0, 1, 3, 2, 5).reshape(CT, 2 * stations, 2 * FRAMES * (FINE // CT))


def correlate(mine, theirs):
    tile_count, signal_count, lanes = theirs.shape
    halfway = lanes // 2
    flipped = jnp.concatenate([-theirs[:, :, halfway:], theirs[:, :, :halfway]], axis=2)
    partner = jnp.stack([theirs, flipped], axis=1)
    product = jnp.einsum("tak,tpbk->tapb", mine, partner, preferred_element_type=jnp.float32)
    local_stations = mine.shape[1] // 2
    block_count = signal_count // mine.shape[1]
    product = product.reshape(tile_count, local_stations, 2, 2, block_count, local_stations, 2)
    product = product.transpose(1, 0, 4, 5, 3, 2, 6).reshape(
        local_stations, tile_count, block_count, local_stations, 8
    )
    return (product * (1.0 / halfway)).astype(jnp.bfloat16)


def drop_autos(tiles_all, block_index):
    local_stations, tile_count, block_count, other_stations, comps = tiles_all.shape
    same_block = jnp.arange(block_count, dtype=jnp.int32) == block_index
    same_station = (
        jnp.arange(local_stations, dtype=jnp.int32)[:, None]
        == jnp.arange(other_stations, dtype=jnp.int32)[None, :]
    )
    matched = same_station[:, None, None, :, None] & same_block[None, None, :, None, None]
    return jnp.where(matched, jnp.zeros_like(tiles_all), tiles_all)


def lookup_taps(index, kernel_table):
    choose = (index[:, None] == jnp.arange(kernel_table.shape[0], dtype=jnp.int32)[None, :]).astype(
        jnp.float32
    )
    return jnp.dot(choose, kernel_table, precision=lax.Precision.HIGHEST).astype(jnp.bfloat16)


def spread_taps(taps, centre, extent):
    cells = jnp.arange(extent, dtype=jnp.int32)[:, None]
    placed = jnp.zeros((extent, taps.shape[1]), jnp.float32)
    for offset in range(KW):
        matched = cells == centre[None, :] + (offset - KW // 2)
        placed = jnp.where(matched, taps[offset][None, :].astype(jnp.float32), placed)
    return placed


def grid_slots(payload, cells):
    slot_count = payload.shape[1]
    values = payload[:8].astype(jnp.float32)
    across = spread_taps(payload[8 : 8 + KW], cells[0], G)
    down = spread_taps(payload[8 + KW : 8 + 2 * KW], cells[1], G).astype(jnp.bfloat16)
    weighted = (
        (values[:, None, :] * across[None, :, :]).astype(jnp.bfloat16).reshape(8 * G, slot_count)
    )
    return lax.dot_general(
        down, weighted, (((1,), (1,)), ((), ())), preferred_element_type=jnp.float32
    )


def grid_in_blocks(payload, cells, block_size):
    pieces = payload.shape[1] // block_size
    payload_blocks = payload.reshape(payload.shape[0], pieces, block_size).transpose(1, 0, 2)
    cell_blocks = cells.reshape(2, pieces, block_size).transpose(1, 0, 2)

    def accumulate(total, pair):
        return (total + grid_slots(pair[0], pair[1]), None)

    total, unused = lax.scan(
        accumulate, jnp.zeros((G, 8 * G), jnp.float32), (payload_blocks, cell_blocks)
    )
    return total


def per_device(
    voltages, prototype, kernel_table, tile_subgrid, tile_cells, tile_offsets, subgrid_slot
):
    spectra = channelize(voltages, prototype)
    rank_here = lax.axis_index("stn")
    result = correlate(spectra, lax.all_gather(spectra, "stn", axis=1, tiled=True))
    visible = drop_autos(result, rank_here)
    values = visible.reshape(-1, 8)
    tile_total = values.shape[0]
    slot_depth = 2 * tile_total // NSUB
    subgrid = tile_subgrid.reshape(-1)
    cells = tile_cells.reshape(-1, 2)
    offsets = tile_offsets.reshape(-1, 2)
    places_index = jnp.arange(NSUB, dtype=jnp.int32)[None, :]
    position = jnp.sum(
        jnp.where(subgrid[:, None] == places_index, subgrid_slot[None, :], 0), axis=1
    )
    member = (position[:, None] == places_index).astype(jnp.int32)
    rank = jnp.sum(member * jnp.cumsum(member, axis=0), axis=1) - 1
    target = position * slot_depth + rank
    across = lookup_taps(offsets[:, 0], kernel_table)
    down = lookup_taps(offsets[:, 1], kernel_table)
    payload = jnp.concatenate([values, across, down], axis=1)
    width_pay = payload.shape[1]
    slot_payload = (
        jnp.zeros((width_pay, NSUB * slot_depth), jnp.bfloat16).at[:, target].set(payload.T)
    )
    slot_cells = jnp.zeros((2, NSUB * slot_depth), jnp.int32).at[:, target].set(cells.T)
    slot_payload = slot_payload.reshape(width_pay, NSUB, slot_depth).transpose(1, 0, 2)
    slot_cells = slot_cells.reshape(2, NSUB, slot_depth).transpose(1, 0, 2)
    groups = lax.axis_size("chan")
    owned_count = NSUB // groups
    payloads = lax.all_to_all(
        slot_payload.reshape(groups, owned_count, width_pay, slot_depth),
        "chan",
        split_axis=0,
        concat_axis=3,
        tiled=True,
    )
    placements = lax.all_to_all(
        slot_cells.reshape(groups, owned_count, 2, slot_depth),
        "chan",
        split_axis=0,
        concat_axis=3,
        tiled=True,
    )

    def one_subgrid(pair):
        return grid_in_blocks(pair[0], pair[1], slot_depth)

    owned = lax.map(one_subgrid, (payloads[0], placements[0]))
    return lax.psum_scatter(owned, "stn", scatter_dimension=2, tiled=True)


def solution(mesh):
    return jax.shard_map(
        per_device,
        mesh=mesh,
        in_specs=(
            P("stn", None, None, "chan", None),
            P(),
            P(),
            P("chan", "stn", None, None, None),
            P("chan", "stn", None, None, None),
            P("chan", "stn", None, None, None),
            P(),
        ),
        out_specs=P("chan", None, "stn"),
        check_vma=False,
    )
```

profile of v0, /device:TPU:32, one launch (start us, length us, event | category | flops | bytes accessed | tf_op | source)
XLA Modules:
  0.0 1447.3 jit_solution(1598610117167969650)
XLA Ops:
  6.5 1.1 sine_multiply_fusion
  7.6 1.0 fusion.81
  8.6 1.2 fusion.86
  9.8 1.0 copy.111
  10.9 0.5 fusion.66
  11.6 0.8 convolution_convert_fusion.2
  12.5 0.8 reshape.633
  13.3 0.5 select_reduce_fusion
  14.5 1.6 broadcast_add_fusion.12
  16.1 2.0 copy.110
  18.1 1.7 fusion.40
  19.9 4.9 copy.123
  24.9 47.4 %scatter_custom_fusion.1 = s32[2,32768]{0,1:T(8,128)} fusion(s32[16384]{0:T(1024)S(1)} %bitcast.210, s32[16384,2]{1,0:T(8,128)} %copy.123, s32[]{:T(128)} %constant.50.clone.1), kind=kCustom, calls=%fused_computation.90 | custom fusion | bytes 262656 | tf_op jit(solution)/shard_map/scatter | solution.py:140
  72.3 9.9 copy.124
  82.2 12.6 all-to-all-start.1
  95.2 0.5 broadcast_in_dim.135
  95.8 0.4 convolution_convert_fusion
  96.2 0.4 convolution_convert_fusion.1
  96.6 36.8 %all-gather.2.cloned.1.call-done = bf16[4,1024,512]{2,1,0:T(8,128)(2,1)} async-done(((bf16[4,16,512]{2,1,0:T(8,128)(2,1)}), bf16[4,1024,512]{2,1,0:T(8,128)(2,1)}) %all-gather.2.cloned.1.call-update) | async-done | bytes 4194320 | tf_op jit(solution)/shard_map/all_gather | solution.py:118
  133.4 2.5 slice_negate_fusion
  136.3 1.8 copy-done.2
  138.1 2.7 fusion.46
  140.8 6.1 copy.115
  146.9 33.5 %copy.116 = bf16[8,4,64,8,2,2,2]{3,2,1,0,6,5,4:T(8,128)(2,1)} copy(bf16[8,4,64,8,2,2,2]{1,6,3,2,4,5,0:T(2,128)(2,1)} %bitcast.175) | data formatting | bytes 524288 | tf_op jit(solution)/shard_map/convert_element_type | solution.py:56
  180.4 10.4 convert_element_type.227
  191.1 3.4 copy.118
  194.5 46.3 %scatter_custom_fusion = bf16[22,32768]{0,1:T(8,128)(2,1)} fusion(s32[16384]{0:T(1024)S(1)} %bitcast.211, bf16[16384,22]{1,0:T(8,128)(2,1)} %copy.118, bf16[]{:T(256)} %constant.57.clone.1), kind=kCustom, calls=%fused_computation.93 | custom fusion | bytes 1442304 | tf_op jit(solution)/shard_map/scatter | solution.py:138
  240.7 7.4 copy.119
  248.2 0.6 reshape.636
  248.7 1.7 copy.120
  250.4 32.0 %all-to-all-start = ((bf16[8,4,22,1024]{3,1,2,0:T(4,128)(2,1)}), bf16[8,4,22,1024]{3,1,2,0:T(4,128)(2,1)S(1)}, u32[]{:S(2)}, u32[]{:S(2)}) async-start(bf16[8,4,22,1024]{3,1,2,0:T(4,128)(2,1)} %copy.120), calls=%async_computation | async-start | bytes 2883584 | tf_op jit(solution)/shard_map/all_to_all | solution.py:145
  282.8 63.8 %all-to-all-done = bf16[8,4,22,1024]{3,1,2,0:T(4,128)(2,1)S(1)} async-done(((bf16[8,4,22,1024]{3,1,2,0:T(4,128)(2,1)}), bf16[8,4,22,1024]{3,1,2,0:T(4,128)(2,1)S(1)}, u32[]{:S(2)}, u32[]{:S(2)}) %all-to-all-start) | async-done | bytes 1441824 | tf_op jit(solution)/shard_map/all_to_all | solution.py:145
  346.6 1.9 copy.129
  348.5 2.1 reshape.689
  350.6 29.1 %while.22 = (s32[]{:T(128)}, f32[4,48,384]{2,1,0:T(8,128)S(1)}, bf16[4,22,8192]{2,1,0:T(8,128)(2,1)S(1)}, s32[4,2,8192]{2,1,0:T(2,128)S(1)}, s32[]{:T(128)}, /*i...) while((s32[]{:T(128)}, f32[4,48,384]{2,1,0:T(8,128)S(1)}, ...), condition=%wide.region_9.10_spmd, body=%wide.region_6.9_spmd.sunk | while | flops 39983120 | bytes 5698380 | solution.py:163
  351.2 6.7 while.23
  351.7 0.4 convolution_add_fusion.2
  352.5 0.4 convolution_add_fusion.2
  353.3 0.4 convolution_add_fusion.2
  354.2 0.4 convolution_add_fusion.2
  355.0 0.4 convolution_add_fusion.2
  355.8 0.4 convolution_add_fusion.2
  357.5 0.4 convolution_add_fusion.2
  358.5 6.7 while.23
  358.9 0.4 convolution_add_fusion.2
  360.6 0.4 convolution_add_fusion.2
  361.4 0.4 convolution_add_fusion.2
  363.1 0.4 convolution_add_fusion.2
  363.9 0.4 convolution_add_fusion.2
  364.8 0.4 convolution_add_fusion.2
  365.8 6.7 while.23
  366.2 0.4 convolution_add_fusion.2
  367.0 0.4 convolution_add_fusion.2
  367.9 0.4 convolution_add_fusion.2
  368.7 0.4 convolution_add_fusion.2
  369.6 0.4 convolution_add_fusion.2
  370.4 0.4 convolution_add_fusion.2
  372.1 0.4 convolution_add_fusion.2
  373.0 6.7 while.23
  373.5 0.4 convolution_add_fusion.2
  379.8 1.2 copy.127
  381.0 1.3 dynamic-slice
  382.9 1056.3 %all-reduce.3.cloned.1.call-done = f32[4,48,384]{1,0,2:T(4,128)} async-done(((f32[4,48,384]{1,0,2:T(4,128)}), f32[4,48,384]{1,0,2:T(4,128)}) %all-reduce.3.cloned.1.call-update) | async-done | bytes 294928
  1439.2 1.3 constant_dynamic-slice_fusion.18
  (305 shorter events, 20.8 us)
Async XLA Ops:
  6.5 89.3 %copy-start = (f32[8,7]{1,0:T(8,128)S(1)}, f32[8,7]{1,0:T(8,128)}, u32[]{:S(2)}) copy-start(f32[8,7]{1,0:T(8,128)} %param.13) | copy-start | bytes 676
  6.5 126.9 %all-gather.2.cloned.1.call-start = ((), (), s32[]{:S(2)}) async-start(), calls=%async_computation.2 | async-start | bytes 4259840 | tf_op jit(solution)/shard_map/all_gather | solution.py:118
  11.4 1.9 copy-start.5
  11.4 1.9 copy-start.6
  18.1 1.7 copy-start.3
  72.3 23.4 %copy-start.4 = (s32[1,8,4,512,2]{3,4,2,1,0:T(2,128)S(1)}, s32[1,8,4,512,2]{3,4,2,1,0:T(2,128)}, u32[]{:S(2)}) copy-start(s32[1,8,4,512,2]{3,4,2,1,0:T(2,128)} %param.16) | copy-start | bytes 393220
  82.2 168.3 %all-to-all-start.1 = ((s32[8,4,2,1024]{3,2,1,0:T(2,128)}), s32[8,4,2,1024]{3,2,1,0:T(2,128)S(1)}, u32[]{:S(2)}, u32[]{:S(2)}) async-start(s32[8,4,2,1024]{3,2,1,0:T(2,128)} %bitcast.44), calls=%async_computation.1 | async-start | bytes 524288 | tf_op jit(solution)/shard_map/all_to_all | solution.py:152
  135.9 2.2 copy-start.2
  250.4 96.2 %all-to-all-start = ((bf16[8,4,22,1024]{3,1,2,0:T(4,128)(2,1)}), bf16[8,4,22,1024]{3,1,2,0:T(4,128)(2,1)S(1)}, u32[]{:S(2)}, u32[]{:S(2)}) async-start(bf16[8,4,22,1024]{3,1,2,0:T(4,128)(2,1)} %copy.120), calls=%async_computation | async-start | bytes 2883584 | tf_op jit(solution)/shard_map/all_to_all | solution.py:145
  282.4 1156.8 %all-reduce.3.cloned.1.call-start = ((), (), s32[]{:S(2)}) async-start(), calls=%async_computation.3 | async-start | bytes 1572864
  379.8 1060.7 %copy-start.1 = (f32[8,7]{1,0:T(8,128)S(1)}, f32[8,7]{1,0:T(8,128)}, u32[]{:S(2)}) copy-start(f32[8,7]{1,0:T(8,128)} %param.13) | copy-start | bytes 676
Sparse Core Ops, SparseCore 0:
  13.4 119.9 all-gather.1
  381.1 1058.0 all-reduce.2
where the time goes:
time: 1450 us
  waiting for transfers between devices  1160 us (80%)
  local copies, waits for them, and re-layouts  191 us (13%)
  starting transfers between devices  44.6 us (3%)
  other arithmetic  21.5 us (1%)
  matrix products  16.5 us (1%)
    unnamed x3, waiting for transfers between devices  1060 us
    all_to_all x1, waiting for transfers between devices, per_device(): lax.all_to_all(slot_payload.reshape(groups, owned_count, width_pay, slot_...  63.8 us
    convert_element_type x3, local copies, waits for them, and re-layouts, correlate(): return (product * (1.0 / halfway)).astype(jnp.bfloat16)  50.1 us
    scatter x1, local copies, waits for them, and re-layouts, per_device(): jnp.zeros((2, NSUB * slot_depth), jnp.int32).at[:, target].set(cells.T)  47.4 us
    scatter x1, local copies, waits for them, and re-layouts, per_device(): jnp.zeros((width_pay, NSUB * slot_depth), jnp.bfloat16).at[:, target]  46.3 us
    all_gather x1, waiting for transfers between devices, per_device(): lax.all_gather(spectra, 'stn', axis=1, tiled=True)  36.8 us
    all_to_all x1, starting transfers between devices, per_device(): lax.all_to_all(slot_payload.reshape(groups, owned_count, width_pay, slot_...  32 us
  transfers between devices with their start and end apart: 4, of which 3 were waited for; matrix products, arithmetic and copies ran while one was open for 13% of the time, Pallas kernels for 0%

commit v1 on v0

v1 whole, which is shorter than its diff:
```python
import math

import jax
import jax.numpy as jnp
from jax import lax
from jax.experimental import pallas as pl
from jax.experimental.pallas import tpu as pltpu
from jax.sharding import Mesh, PartitionSpec as P

FINE = 256
TAPS = 16
FRAMES = 4
CT = 4
CB = FINE // CT
STN_DEV = 8
STATIONS = 512
G = 48
NSUB = 32
KW = 7
OS = 8
SIDE = 768
STN = ("x", "y", "zh", "core")


def fourier_table(length):
    index = jnp.arange(length, dtype=jnp.int32)
    phase = index[:, None] * index[None, :] % length
    angle = phase.astype(jnp.float32) * (2.0 * math.pi / length)
    cosine = jnp.cos(angle) / math.sqrt(length)
    sine = jnp.sin(angle) / math.sqrt(length)
    upper = jnp.concatenate([cosine, -sine], axis=1)
    lower = jnp.concatenate([sine, cosine], axis=1)
    return jnp.concatenate([upper, lower], axis=0)


def channelize(voltages, prototype):
    stations = voltages.shape[0]
    samples = (
        voltages[:, :, :, 0, :].astype(jnp.float32).reshape(stations, 2, 2, FRAMES + TAPS - 1, FINE)
    )
    filtered = jnp.zeros((stations, 2, 2, FRAMES, FINE), jnp.float32)
    for tap in range(TAPS):
        filtered = filtered + prototype[tap] * samples[:, :, :, tap : tap + FRAMES, :]
    frame_rows = filtered.transpose(0, 1, 3, 2, 4).reshape(stations * 2 * FRAMES, 2 * FINE)
    spectra = jnp.dot(frame_rows, fourier_table(FINE), precision=lax.Precision.HIGHEST).astype(
        jnp.bfloat16
    )
    spectra = spectra.reshape(stations, 2, FRAMES, 2, CT, CB)
    return spectra.transpose(4, 1, 0, 3, 2, 5).reshape(CT, 2, stations, 2 * FRAMES * CB)


def grid_body(table, index, urow, lhs, rhs, send, keep, vis, taps, amat, wmat):
    step = pl.program_id(0)

    @pl.when(step == 0)
    def _():
        send[...] = jnp.zeros_like(send)
        keep[...] = jnp.zeros_like(keep)

    product = lax.dot_general(
        lhs[0], rhs[0], (((1,), (1,)), ((), ())), preferred_element_type=jnp.float32
    )
    product = (product * (1.0 / (FRAMES * CB))).astype(jnp.bfloat16).astype(jnp.float32)
    vis[...] = product.reshape(4, STN_DEV, 2 * STATIONS)
    for axis in range(2):
        chosen = index[0, 3 + axis]
        masks = [chosen == o for o in range(1, OS)]
        for k in range(KW):
            value = jnp.full((STN_DEV, STATIONS), table[0, k], jnp.float32)
            for o in range(1, OS):
                value = jnp.where(masks[o - 1], table[o, k], value)
            taps[axis * KW + k] = value

    def one_station(a, carry):
        row = pl.ds(a, 1)
        position = index[0, 0, row, :]
        u0 = index[0, 1, row, :] + 64 * (position & 1) - KW // 2
        v0 = index[0, 2, row, :] - KW // 2
        high = position >> 1
        shape = (G, STATIONS)
        away = lax.broadcasted_iota(jnp.int32, shape, 0) - v0
        down = jnp.zeros(shape, jnp.float32)
        for k in range(KW):
            down = jnp.where(away == k, taps[KW + k, row, :], down)
        for h in range(NSUB // 2):
            amat[h * G : (h + 1) * G, :] = jnp.where(high == h, down, 0.0).astype(jnp.bfloat16)
        for half in range(2):
            away = urow[half * G : (half + 1) * G, :] - u0
            across = jnp.zeros(shape, jnp.float32)
            for k in range(KW):
                across = jnp.where(away == k, taps[k, row, :], across)
            for j in range(8):
                value = vis[j // 2, row, (j % 2) * STATIONS : (j % 2 + 1) * STATIONS]
                first = half * 8 * G + j * G
                wmat[first : first + G, :] = (value * across).astype(jnp.bfloat16)
        nt = (((1,), (1,)), ((), ()))
        total = lax.dot_general(
            wmat[...], amat[...], nt, preferred_element_type=jnp.float32
        )
        send[...] += total[: SIDE // 2]
        keep[...] += total[SIDE // 2 :]
        return carry

    lax.fori_loop(0, STN_DEV, one_station, 0)


def grid_tiles(table, index, urow, lhs, rhs):
    half = jax.ShapeDtypeStruct((SIDE // 2, SIDE), jnp.float32)
    whole = pl.BlockSpec((SIDE // 2, SIDE), lambda t: (0, 0))
    return pl.pallas_call(
        grid_body,
        grid=(CT,),
        in_specs=[
            pl.BlockSpec(memory_space=pltpu.SMEM),
            pl.BlockSpec((1, 5, STN_DEV, STATIONS), lambda t: (t, 0, 0, 0)),
            pl.BlockSpec((2 * G, STATIONS), lambda t: (0, 0)),
            pl.BlockSpec((1, 4 * STN_DEV, 2 * FRAMES * CB), lambda t: (t, 0, 0)),
            pl.BlockSpec((1, 2 * STATIONS, 2 * FRAMES * CB), lambda t: (t, 0, 0)),
        ],
        out_specs=[whole, whole],
        out_shape=[half, half],
        scratch_shapes=[
            pltpu.VMEM((4, STN_DEV, 2 * STATIONS), jnp.float32),
            pltpu.VMEM((2 * KW, STN_DEV, STATIONS), jnp.float32),
            pltpu.VMEM((SIDE, STATIONS), jnp.bfloat16),
            pltpu.VMEM((SIDE, STATIONS), jnp.bfloat16),
        ],
    )(table, index, urow, lhs, rhs)


def per_device(
    voltages, prototype, kernel_table, tile_subgrid, tile_cells, tile_offsets, subgrid_slot
):
    spectra = channelize(voltages, prototype)
    theirs = lax.all_gather(spectra, STN, axis=2, tiled=True).reshape(
        CT, 2 * STATIONS, 2 * FRAMES * CB
    )
    lanes = FRAMES * CB
    turned = jnp.concatenate([spectra[..., lanes:], -spectra[..., :lanes]], axis=-1)
    lhs = jnp.stack([spectra, turned], axis=1).reshape(CT, 4 * STN_DEV, 2 * lanes)

    core = lax.axis_index("core")
    subgrid = tile_subgrid.reshape(STN_DEV, CT, STATIONS)
    places = jnp.arange(NSUB, dtype=jnp.int32)
    position = jnp.sum(
        jnp.where(subgrid[..., None] == places, subgrid_slot, 0), axis=-1
    )
    mine = lax.axis_index(STN) * STN_DEV + jnp.arange(STN_DEV, dtype=jnp.int32)
    station = jnp.arange(STATIONS, dtype=jnp.int32)
    position = jnp.where(mine[:, None, None] == station, -1, position)
    cells = tile_cells.reshape(STN_DEV, CT, STATIONS, 2)
    offsets = tile_offsets.reshape(STN_DEV, CT, STATIONS, 2)
    index = jnp.stack(
        [position, cells[..., 0], cells[..., 1], offsets[..., 0], offsets[..., 1]], axis=0
    ).transpose(2, 0, 1, 3)
    r = jnp.arange(G, dtype=jnp.int32)
    base = (r // 24) * 24 + (r // 12) % 2 * 12 + r % 6 + 64 * ((r // 6) % 2)
    urow = jnp.concatenate([base + 6 * (1 - core), base + 6 * core])
    urow = jnp.broadcast_to(urow[:, None], (2 * G, STATIONS))
    table = lax.reduce_precision(kernel_table, 8, 7)

    send, keep = grid_tiles(table, index, urow, lhs, theirs)
    total = keep + lax.ppermute(send, "core", [(0, 1), (1, 0)])
    for axis in ("x", "y"):
        total = total.reshape(4, -1, SIDE)
        total = jnp.sum(lax.all_to_all(total, axis, 0, 0, tiled=True), axis=0)
    total = total.reshape(2, 12, 8, 96).transpose(0, 2, 1, 3).reshape(16, 12, 96)
    total = jnp.sum(lax.all_to_all(total, ("zh", "chan"), 0, 0, tiled=True), axis=0)
    total = total.reshape(2, 6, 2, G)
    return total.transpose(2, 0, 3, 1).reshape(4, G, 6)


def solution(mesh):
    fine = Mesh(mesh.devices.reshape(4, 4, 2, 2, 8), STN + ("chan",))
    return jax.shard_map(
        per_device,
        mesh=fine,
        in_specs=(
            P(STN, None, None, "chan", None),
            P(),
            P(),
            P("chan", STN, None, None, None),
            P("chan", STN, None, None, None),
            P("chan", STN, None, None, None),
            P(),
        ),
        out_specs=P("chan", None, STN),
        check_vma=False,
    )
```

time: 1450 us -> 248 us (0.17)
  waiting for transfers between devices: 1160 us -> 133 us
  local copies, waits for them, and re-layouts: 191 us -> 5.85 us
  blocking collectives: 0 us -> 53.3 us
  starting transfers between devices: 44.6 us -> 2.14 us
  Pallas kernels: 0 us -> 32.7 us
  matrix products: 16.5 us -> 0.75 us
  other arithmetic: 21.5 us -> 6.23 us
    unnamed x3 -> x1, waiting for transfers between devices: 1060 us -> 0.02 us
    scatter x2 -> x0, local copies, waits for them, and re-layouts: 93.7 us -> none  [the longest x1 47.4 us: per_device(): jnp.zeros((2, NSUB * slot_depth), jnp.int32).at[:, target].set(cells.T)]
    all_gather x1, waiting for transfers between devices: 36.8 us -> 130 us  [per_device(): lax.all_gather(spectra, STN, axis=2, tiled=True)]
    all_to_all x2 -> x0, waiting for transfers between devices: 63.8 us -> none  [the longest x1 63.8 us: per_device(): lax.all_to_all(slot_payload.reshape(groups, owned_count, width_pay, slot_...]
    all_to_all x0 -> x3, blocking collectives: none -> 53.3 us  [the longest x2 29.9 us: per_device(): total = jnp.sum(lax.all_to_all(total, axis, 0, 0, tiled=True), axis=0)]
    convert_element_type x3 -> x0, local copies, waits for them, and re-layouts: 50.1 us -> none  [correlate(): return (product * (1.0 / halfway)).astype(jnp.bfloat16)]
    all_to_all x2 -> x0, starting transfers between devices: 44.6 us -> none  [the longest x1 32 us: per_device(): lax.all_to_all(slot_payload.reshape(groups, owned_count, width_pay, slot_...]
    pallas_call x0 -> x1, Pallas kernels: none -> 32.7 us  [grid_tiles(): pl.pallas_call(grid_body, grid=(CT,), in_specs=[pl.BlockSpec(memory_space...]
  transfers between devices with their start and end apart: 4 -> 2, of which waited for: 3 -> 2; matrix products, arithmetic and copies ran while one was open for 13% -> 1% of each run, Pallas kernels for 0% -> 0%
where the time goes in v1:
time: 248 us
  waiting for transfers between devices  133 us (54%)
  blocking collectives  53.3 us (21%)
  Pallas kernels  32.7 us (13%)
  between operations  13.6 us (5%)
  other arithmetic  6.23 us (3%)
  local copies, waits for them, and re-layouts  5.85 us (2%)
    all_gather x1, waiting for transfers between devices, per_device(): lax.all_gather(spectra, STN, axis=2, tiled=True)  130 us
    pallas_call x1, Pallas kernels, grid_tiles(): pl.pallas_call(grid_body, grid=(CT,), in_specs=[pl.BlockSpec(memory_space...  32.7 us
    all_to_all x2, blocking collectives, per_device(): total = jnp.sum(lax.all_to_all(total, axis, 0, 0, tiled=True), axis=0)  29.9 us
    all_to_all x1, blocking collectives, per_device(): lax.all_to_all(total, ('zh', 'chan'), 0, 0, tiled=True)  23.4 us
  transfers between devices with their start and end apart: 2, of which 2 were waited for; matrix products, arithmetic and copies ran while one was open for 1% of the time, Pallas kernels for 0%

profile of v1, /device:TPU:32, one launch (start us, length us, event | category | flops | bytes accessed | tf_op | source)
XLA Modules:
  0.0 247.7 jit_solution(3549282743054244914)
XLA Ops:
  6.5 0.0 all-gather.2.cloned.1.call-start
  6.5 1.0 fusion.29
  7.5 1.1 sine_multiply_fusion
  8.6 1.1 fusion.46
  9.6 1.0 copy.52
  10.6 0.1 reshape.107
  10.8 0.5 fusion.14
  11.3 0.0 copy-start.4
  11.3 0.0 copy-start.3
  11.3 0.0 copy-start.1
  11.3 0.0 copy-start.2
  11.3 0.1 copy.53
  11.4 0.0 copy-start.5
  11.5 0.8 convolution_convert_fusion
  12.2 0.1 reshape.97
  12.3 0.1 copy.54
  12.4 0.8 reshape.98
  13.2 0.0 all-gather.2.cloned.1.call-update
  13.2 0.1 stack_reshape.3
  13.4 0.0 copy-done.4
  13.4 0.6 reduce_precision.3.table
  14.0 0.0 copy-done.3
  14.0 0.0 copy-done.1
  14.0 0.1 copy.68
  14.1 0.0 copy-done.2
  14.1 0.1 copy.67
  14.2 0.8 fusion.45
  15.0 0.7 copy.56
  15.7 0.1 pad_add_fusion
  15.8 0.0 copy-done.5
  15.8 0.5 select_reduce_fusion
  16.3 0.1 iota_compare_fusion.1
  16.5 0.0 copy-start
  16.5 130.3 %all-gather.2.cloned.1.call-done = bf16[4,2,512,512]{3,2,1,0:T(8,128)(2,1)} async-done(((bf16[4,2,8,512]{3,2,1,0:T(8,128)(2,1)}), bf16[4,2,512,512]{3,2,1,0:T(8,128)(2,1)}) %all-gather.2.cloned.1.call-update) | async-done | bytes 4194320 | tf_op jit(solution)/shard_map/all_gather | solution.py:135
  146.8 0.7 broadcast_in_dim.35.urow
  147.5 0.0 copy-done
  147.5 32.7 %shard_map.73 = (f32[384,768]{1,0:T(8,128)}, f32[384,768]{1,0:T(8,128)}) custom-call(f32[8,7]{1,0:T(8,128)} %reduce_precision.3.table, s32[4,5,8,512]{3,2,1,0:T(8,128)} %bitcast.84, s32[96,512]{1,0:T(8,128)} %broadcast_in_dim.35.urow, bf16[4,32,512]{2,1,0:T(8,128)(2,1)} %bitcast.77, bf16[4,1024,512]{2,1,0:T(8,128)(2,1)} %bitcast.75), custom_call_target="tpu_custom_call" | custom-call | tf_op jit(solution)/shard_map/pallas_call | solution.py:110
  180.2 2.1 collective-permute-start
  182.4 2.8 %collective-permute-done = f32[384,768]{1,0:T(8,128)S(1)} collective-permute-done((f32[384,768]{1,0:T(8,128)}, f32[384,768]{1,0:T(8,128)S(1)}, u32[]{:S(2)}, u32[]{:S(2)}) %collective-permute-start) | collective-permute-done | bytes 1179680 | tf_op jit(solution)/shard_map/ppermute | solution.py:163
  185.2 1.4 add.160
  186.6 19.6 %all_to_all.15 = f32[4,96,768]{2,1,0:T(8,128)S(1)} all-to-all(f32[4,96,768]{2,1,0:T(8,128)S(1)} %bitcast.74), channel_id=1, replica_groups=mesh['x'=4,'y'=4,'zh'=2,'core'=2,'chan'=8] {'x'}, dimensions={0} | all-to-all | bytes 2359296 | tf_op jit(solution)/shard_map/all_to_all | solution.py:166
  206.2 0.1 reduce_sum.40
  206.3 10.3 %all_to_all.16 = f32[4,24,768]{2,1,0:T(8,128)S(1)} all-to-all(f32[4,24,768]{2,1,0:T(8,128)S(1)} %bitcast.76), channel_id=1, replica_groups=mesh['x'=4,'y'=4,'zh'=2,'core'=2,'chan'=8] {'y'}, dimensions={0} | all-to-all | bytes 589824 | tf_op jit(solution)/shard_map/all_to_all | solution.py:166
  216.6 0.1 reshape.103
  216.7 23.4 %all_to_all.17 = f32[16,12,96]{2,1,0:T(8,128)S(1)} all-to-all(f32[16,12,96]{2,1,0:T(8,128)S(1)} %copy.58), channel_id=1, replica_groups=mesh['x'=4,'y'=4,'zh'=2,'core'=2,'chan'=8] {'zh','chan'}, dimensions={0} | all-to-all | bytes 147456 | tf_op jit(solution)/shard_map/all_to_all | solution.py:168
  240.2 0.1 reshape.105
  240.3 0.6 copy.59
  (15 shorter events, 0.2 us)
Async XLA Ops:
  6.5 140.2 %all-gather.2.cloned.1.call-start = ((), (), s32[]{:S(2)}) async-start(), calls=%async_computation.3 | async-start | bytes 4259840 | tf_op jit(solution)/shard_map/all_gather | solution.py:135
  11.3 2.1 copy-start.4
  11.3 2.7 %copy-start.3 = (s32[1,8,4,512,1]{3,4,2,1,0:T(1,128)S(1)}, s32[1,8,4,512,1]{3,4,2,1,0:T(1,128)}, u32[]{:S(2)}) copy-start(s32[1,8,4,512,1]{3,4,2,1,0:T(1,128)} %param.10) | copy-start | bytes 196612
  11.3 2.7 %copy-start.1 = (s32[1,8,4,512,2]{3,4,2,1,0:T(2,128)S(1)}, s32[1,8,4,512,2]{3,4,2,1,0:T(2,128)}, u32[]{:S(2)}) copy-start(s32[1,8,4,512,2]{3,4,2,1,0:T(2,128)} %param.11) | copy-start | bytes 393220
  11.3 2.8 %copy-start.2 = (s32[1,8,4,512,2]{3,4,2,1,0:T(2,128)S(1)}, s32[1,8,4,512,2]{3,4,2,1,0:T(2,128)}, u32[]{:S(2)}) copy-start(s32[1,8,4,512,2]{3,4,2,1,0:T(2,128)} %param.12) | copy-start | bytes 393220
  11.4 4.3 %copy-start.5 = (s32[32]{0:T(128)S(1)}, s32[32]{0:T(128)}, u32[]{:S(2)}) copy-start(s32[32]{0:T(128)} %param.13) | copy-start | bytes 388
  16.5 131.1 %copy-start = (s32[5,8,4,512]{3,1,0,2:T(8,128)}, s32[5,8,4,512]{3,1,0,2:T(8,128)S(1)}, u32[]{:S(2)}) copy-start(s32[5,8,4,512]{3,1,0,2:T(8,128)S(1)} %fusion.30) | copy-start | bytes 983044
  180.2 4.9 %collective-permute-start = (f32[384,768]{1,0:T(8,128)}, f32[384,768]{1,0:T(8,128)S(1)}, u32[]{:S(2)}, u32[]{:S(2)}) collective-permute-start(f32[384,768]{1,0:T(8,128)} %get-tuple-element.8), channel_id=1, source_target_pairs={{0,8},{8,0},{1,9},{9,1},{2,10},{10,2},{3,11},{11,3},{4,12},{12,4},... | collective-permute-start | bytes 3538952 | tf_op jit(solution)/shard_map/ppermute | solution.py:163
Sparse Core Ops, SparseCore 0:
  13.3 133.4 all-gather.1

commit v2 on v1

v2 whole, which is shorter than its diff:
```python
import math

import jax
import jax.numpy as jnp
from jax import lax
from jax.experimental import pallas as pl
from jax.experimental.pallas import tpu as pltpu
from jax.sharding import Mesh, PartitionSpec as P

FINE = 256
TAPS = 16
FRAMES = 4
CT = 4
CB = FINE // CT
STN_DEV = 8
STATIONS = 512
G = 48
NSUB = 32
KW = 7
OS = 8
SIDE = 768
PART = 256
BUNCH = 2
STN = ("x", "y", "zh", "core")


def fourier_table(length):
    index = jnp.arange(length, dtype=jnp.int32)
    phase = index[:, None] * index[None, :] % length
    angle = phase.astype(jnp.float32) * (2.0 * math.pi / length)
    cosine = jnp.cos(angle) / math.sqrt(length)
    sine = jnp.sin(angle) / math.sqrt(length)
    upper = jnp.concatenate([cosine, -sine], axis=1)
    lower = jnp.concatenate([sine, cosine], axis=1)
    return jnp.concatenate([upper, lower], axis=0)


def channelize(voltages, prototype):
    stations = voltages.shape[0]
    samples = (
        voltages[:, :, :, 0, :].astype(jnp.float32).reshape(stations, 2, 2, FRAMES + TAPS - 1, FINE)
    )
    filtered = jnp.zeros((stations, 2, 2, FRAMES, FINE), jnp.float32)
    for tap in range(TAPS):
        filtered = filtered + prototype[tap] * samples[:, :, :, tap : tap + FRAMES, :]
    frame_rows = filtered.transpose(0, 1, 3, 2, 4).reshape(stations * 2 * FRAMES, 2 * FINE)
    spectra = jnp.dot(frame_rows, fourier_table(FINE), precision=lax.Precision.HIGHEST).astype(
        jnp.bfloat16
    )
    spectra = spectra.reshape(stations, 2, FRAMES, 2, CT, CB)
    return spectra.transpose(4, 1, 0, 3, 2, 5).reshape(CT, 2, stations, 2 * FRAMES * CB)


def grid_body(
    table, index, urow, lhs, near, far, send_in, keep_in, send, keep, vis, taps, amat, wmat
):
    step = pl.program_id(0)

    @pl.when(step == 0)
    def _():
        send[...] = send_in[...]
        keep[...] = keep_in[...]

    width = PART // 2
    for side, rhs in enumerate((near, far)):
        product = lax.dot_general(
            lhs[0], rhs[0], (((1,), (1,)), ((), ())), preferred_element_type=jnp.float32
        )
        product = (product * (1.0 / (FRAMES * CB))).astype(jnp.bfloat16).astype(jnp.float32)
        product = product.reshape(4, STN_DEV, 2 * width)
        for q in range(2):
            first = q * PART + side * width
            vis[:, :, first : first + width] = product[:, :, q * width : (q + 1) * width]
    for axis in range(2):
        chosen = index[0, 3 + axis]
        masks = [chosen == o for o in range(1, OS)]
        for k in range(KW):
            value = jnp.full((STN_DEV, PART), table[0, k], jnp.float32)
            for o in range(1, OS):
                value = jnp.where(masks[o - 1], table[o, k], value)
            taps[axis * KW + k] = value

    def stations(turn, carry):
        for inner in range(BUNCH):
            row = pl.ds(turn * BUNCH + inner, 1)
            lanes = slice(inner * PART, (inner + 1) * PART)
            position = index[0, 0, row, :]
            u0 = index[0, 1, row, :] + 64 * (position & 1) - KW // 2
            v0 = index[0, 2, row, :] - KW // 2
            high = position >> 1
            shape = (G, PART)
            away = lax.broadcasted_iota(jnp.int32, shape, 0) - v0
            down = jnp.zeros(shape, jnp.float32)
            for k in range(KW):
                down = jnp.where(away == k, taps[KW + k, row, :], down)
            for h in range(NSUB // 2):
                amat[h * G : (h + 1) * G, lanes] = jnp.where(high == h, down, 0.0).astype(
                    jnp.bfloat16
                )
            for half in range(2):
                away = urow[half * G : (half + 1) * G, :] - u0
                across = jnp.zeros(shape, jnp.float32)
                for k in range(KW):
                    across = jnp.where(away == k, taps[k, row, :], across)
                for j in range(8):
                    value = vis[j // 2, row, (j % 2) * PART : (j % 2 + 1) * PART]
                    first = half * 8 * G + j * G
                    wmat[first : first + G, lanes] = (value * across).astype(jnp.bfloat16)
        total = lax.dot_general(
            wmat[...], amat[...], (((1,), (1,)), ((), ())), preferred_element_type=jnp.float32
        )
        send[...] += total[: SIDE // 2]
        keep[...] += total[SIDE // 2 :]
        return carry

    lax.fori_loop(0, STN_DEV // BUNCH, stations, 0)


def grid_tiles(table, index, urow, lhs, near, far, send, keep, part):
    half = jax.ShapeDtypeStruct((SIDE // 2, SIDE), jnp.float32)
    whole = pl.BlockSpec((SIDE // 2, SIDE), lambda t: (0, 0))
    lanes = 2 * FRAMES * CB
    piece = pl.BlockSpec((1, PART, lanes), lambda t: (t, 0, 0))
    return pl.pallas_call(
        grid_body,
        grid=(CT,),
        in_specs=[
            pl.BlockSpec(memory_space=pltpu.SMEM),
            pl.BlockSpec((1, 5, STN_DEV, PART), lambda t: (t, 0, 0, part)),
            pl.BlockSpec((2 * G, PART), lambda t: (0, 0)),
            pl.BlockSpec((1, 4 * STN_DEV, lanes), lambda t: (t, 0, 0)),
            piece,
            piece,
            whole,
            whole,
        ],
        out_specs=[whole, whole],
        out_shape=[half, half],
        input_output_aliases={6: 0, 7: 1},
        scratch_shapes=[
            pltpu.VMEM((4, STN_DEV, 2 * PART), jnp.float32),
            pltpu.VMEM((2 * KW, STN_DEV, PART), jnp.float32),
            pltpu.VMEM((SIDE, BUNCH * PART), jnp.bfloat16),
            pltpu.VMEM((SIDE, BUNCH * PART), jnp.bfloat16),
        ],
    )(table, index, urow, lhs, near, far, send, keep)


def spread_over_plane(spectra):
    copies = jnp.broadcast_to(spectra, (16,) + spectra.shape)
    pieces = lax.all_to_all(copies, ("x", "y"), 0, 0, tiled=True)
    near = pieces.transpose(1, 2, 0, 3, 4).reshape(CT, PART, 2 * FRAMES * CB)
    return near, lax.ppermute(near, "core", [(0, 1), (1, 0)])


def arrival_order():
    slot = jnp.arange(STATIONS, dtype=jnp.int32)
    zh = lax.axis_index("zh") ^ (slot // 256)
    core = lax.axis_index("core") ^ (slot // 128 % 2)
    return ((slot // 8 % 16) * 4 + zh * 2 + core) * STN_DEV + slot % 8


def per_device(
    voltages, prototype, kernel_table, tile_subgrid, tile_cells, tile_offsets, subgrid_slot
):
    swap = [(0, 1), (1, 0)]
    spectra = channelize(voltages, prototype)
    other = lax.ppermute(spectra, "zh", swap)
    parts = (spread_over_plane(spectra), spread_over_plane(other))
    lanes = FRAMES * CB
    turned = jnp.concatenate([spectra[..., lanes:], -spectra[..., :lanes]], axis=-1)
    lhs = jnp.stack([spectra, turned], axis=1).reshape(CT, 4 * STN_DEV, 2 * lanes)

    core = lax.axis_index("core")
    subgrid = tile_subgrid.reshape(STN_DEV, CT, STATIONS)
    places = jnp.arange(NSUB, dtype=jnp.int32)
    position = jnp.sum(
        jnp.where(subgrid[..., None] == places, subgrid_slot, 0), axis=-1
    )
    mine = lax.axis_index(STN) * STN_DEV + jnp.arange(STN_DEV, dtype=jnp.int32)
    station = jnp.arange(STATIONS, dtype=jnp.int32)
    position = jnp.where(mine[:, None, None] == station, -1, position)
    cells = tile_cells.reshape(STN_DEV, CT, STATIONS, 2)
    offsets = tile_offsets.reshape(STN_DEV, CT, STATIONS, 2)
    index = jnp.stack(
        [position, cells[..., 0], cells[..., 1], offsets[..., 0], offsets[..., 1]], axis=0
    ).transpose(2, 0, 1, 3)
    chosen = (station[:, None] == arrival_order()[None, :]).astype(jnp.bfloat16)
    index = jnp.dot(
        index.reshape(-1, STATIONS).astype(jnp.bfloat16),
        chosen,
        preferred_element_type=jnp.float32,
    )
    index = index.astype(jnp.int32).reshape(CT, 5, STN_DEV, STATIONS)
    r = jnp.arange(G, dtype=jnp.int32)
    base = (r // 24) * 24 + (r // 12) % 2 * 12 + r % 6 + 64 * ((r // 6) % 2)
    urow = jnp.concatenate([base + 6 * (1 - core), base + 6 * core])
    urow = jnp.broadcast_to(urow[:, None], (2 * G, PART))
    table = lax.reduce_precision(kernel_table, 8, 7)

    send = jnp.zeros((SIDE // 2, SIDE), jnp.float32)
    keep = jnp.zeros((SIDE // 2, SIDE), jnp.float32)
    for part, (near, far) in enumerate(parts):
        send, keep = grid_tiles(table, index, urow, lhs, near, far, send, keep, part)
    total = keep + lax.ppermute(send.astype(jnp.bfloat16), "core", swap).astype(jnp.float32)
    total = total.astype(jnp.bfloat16).reshape(16, 24, SIDE)
    total = lax.all_to_all(total, ("x", "y"), 0, 0, tiled=True)
    total = jnp.sum(total.astype(jnp.float32), axis=0)
    total = total.reshape(2, 12, 8, 96).transpose(0, 2, 1, 3).reshape(16, 12, 96)
    total = jnp.sum(lax.all_to_all(total, ("zh", "chan"), 0, 0, tiled=True), axis=0)
    total = total.reshape(2, 6, 2, G)
    return total.transpose(2, 0, 3, 1).reshape(4, G, 6)


def solution(mesh):
    fine = Mesh(mesh.devices.reshape(4, 4, 2, 2, 8), STN + ("chan",))
    return jax.shard_map(
        per_device,
        mesh=fine,
        in_specs=(
            P(STN, None, None, "chan", None),
            P(),
            P(),
            P("chan", STN, None, None, None),
            P("chan", STN, None, None, None),
            P("chan", STN, None, None, None),
            P(),
        ),
        out_specs=P("chan", None, STN),
        check_vma=False,
    )
```

time: 248 us -> 155 us (0.62)
  waiting for transfers between devices: 133 us -> 15.2 us
  starting transfers between devices: 2.14 us -> 34.6 us
  between operations: 13.6 us -> 0.28 us
  blocking collectives: 53.3 us -> 42.6 us
  local copies, waits for them, and re-layouts: 5.85 us -> 14 us
  Pallas kernels: 32.7 us -> 37.4 us
    all_gather x1 -> x0, waiting for transfers between devices: 130 us -> none  [per_device(): lax.all_gather(spectra, STN, axis=2, tiled=True)]
    ppermute x1 -> x4, starting transfers between devices: 2.14 us -> 21.1 us  [the longest x1 14.8 us: per_device(): other = lax.ppermute(spectra, 'zh', swap)]
    all_to_all x2 -> x1, blocking collectives: 29.9 us -> 16.1 us  [per_device(): total = lax.all_to_all(total, ('x', 'y'), 0, 0, tiled=True)]
    all_to_all x0 -> x2, starting transfers between devices: none -> 13.5 us  [spread_over_plane(): pieces = lax.all_to_all(copies, ('x', 'y'), 0, 0, tiled=True)]
    all_to_all x0 -> x2, waiting for transfers between devices: none -> 10.8 us  [spread_over_plane(): pieces = lax.all_to_all(copies, ('x', 'y'), 0, 0, tiled=True)]
    pallas_call x1 -> x2, Pallas kernels: 32.7 us -> 37.4 us  [grid_tiles(): pl.pallas_call(grid_body, grid=(CT,), in_specs=[pl.BlockSpec(memory_space...]
    all_to_all x1, blocking collectives: 23.4 us -> 26.4 us  [per_device(): lax.all_to_all(total, ('zh', 'chan'), 0, 0, tiled=True)]
    unnamed x19 -> x23, local copies, waits for them, and re-layouts: 0.25 us -> 2.89 us
  transfers between devices with their start and end apart: 2 -> 6, of which waited for: 2 -> 3; matrix products, arithmetic and copies ran while one was open for 1% -> 8% of each run, Pallas kernels for 0% -> 12%
where the time goes in v2:
time: 155 us; the launch traced here: 154 us
  blocking collectives  42.6 us (27%)
  Pallas kernels  37.4 us (24%)
  starting transfers between devices  34.6 us (22%)
  waiting for transfers between devices  15.2 us (10%)
  local copies, waits for them, and re-layouts  14 us (9%)
  other arithmetic  6.91 us (4%)
  matrix products  2.76 us (2%)
    pallas_call x2, Pallas kernels, grid_tiles(): pl.pallas_call(grid_body, grid=(CT,), in_specs=[pl.BlockSpec(memory_space...  37.4 us
    all_to_all x1, blocking collectives, per_device(): lax.all_to_all(total, ('zh', 'chan'), 0, 0, tiled=True)  26.4 us
    all_to_all x1, blocking collectives, per_device(): total = lax.all_to_all(total, ('x', 'y'), 0, 0, tiled=True)  16.1 us
    ppermute x1, starting transfers between devices, per_device(): other = lax.ppermute(spectra, 'zh', swap)  14.8 us
    all_to_all x2, starting transfers between devices, spread_over_plane(): pieces = lax.all_to_all(copies, ('x', 'y'), 0, 0, tiled=True)  13.5 us
    all_to_all x2, waiting for transfers between devices, spread_over_plane(): pieces = lax.all_to_all(copies, ('x', 'y'), 0, 0, tiled=True)  10.8 us
    ppermute x2, starting transfers between devices, spread_over_plane(): return (near, lax.ppermute(near, 'core', [(0, 1), (1, 0)]))  3.84 us
  transfers between devices with their start and end apart: 6, of which 3 were waited for; matrix products, arithmetic and copies ran while one was open for 8% of the time, Pallas kernels for 12%

profile of v2, /device:TPU:32, one launch (start us, length us, event | category | flops | bytes accessed | tf_op | source)
XLA Modules:
  0.0 153.8 jit_solution(5120464897509834540)
XLA Ops:
  0.0 1.1 sine_multiply_fusion
  1.1 1.0 fusion.30
  2.0 1.1 fusion.70
  3.1 1.0 copy.49
  4.1 0.1 reshape.181
  4.2 0.5 fusion.15
  4.7 0.1 copy.50
  4.9 0.8 convolution_convert_fusion.1
  5.6 0.1 reshape.169
  5.8 0.1 copy.51
  5.8 0.1 reshape.170
  6.0 1.1 broadcast_in_dim.45
  7.1 7.2 %all-to-all-start.1 = ((bf16[16,4,2,8,512]{4,3,2,1,0:T(8,128)(2,1)}), bf16[16,4,2,8,512]{4,3,2,1,0:T(8,128)(2,1)S(1)}, u32[]{:S(2)}, u32[]{:S(2)}) async-start(bf16[16,4,2,8,512]{4,3,2,1,0:T(8,128)(2,1)} %broadcast_in_dim.45), calls=%async_computation.1 | async-start | bytes 2097152 | tf_op jit(solution)/shard_map/all_to_all | solution.py:151
  14.2 14.8 %collective-permute-start = (bf16[4,2,8,512]{3,2,1,0:T(8,128)(2,1)S(1)}, bf16[4,2,8,512]{3,2,1,0:T(8,128)(2,1)S(1)}, u32[]{:S(2)}, u32[]{:S(2)}) collective-permute-start(bf16[4,2,8,512]{3,2,1,0:T(8,128)(2,1)S(1)} %reshape.170), channel_id=1, source_target_pairs={{0,16},{16,0},{1,17},{17,1},{2,18},{18,2},{3,19},{19,3},{4,20},{20... | collective-permute-start | bytes 196616 | tf_op jit(solution)/shard_map/ppermute | solution.py:168
  29.1 0.0 copy-done.6
  29.2 0.1 iota_compare_fusion.3
  29.2 0.0 copy-done.4
  29.3 0.0 copy-done.8
  29.3 0.5 select_reduce_fusion
  29.8 2.8 %collective-permute-done = bf16[4,2,8,512]{3,2,1,0:T(8,128)(2,1)S(1)} collective-permute-done((bf16[4,2,8,512]{3,2,1,0:T(8,128)(2,1)S(1)}, bf16[4,2,8,512]{3,2,1,0:T(8,128)(2,1)S(1)}, u32[]{:S(2)}, u32[]{:S(2)}) %collective-permute-start) | collective-permute-done | bytes 65568 | tf_op jit(solution)/shard_map/ppermute | solution.py:168
  32.6 0.0 all-to-all-done.1
  32.6 1.1 broadcast_in_dim.44
  33.7 6.4 %all-to-all-start = ((bf16[16,4,2,8,512]{4,3,2,1,0:T(8,128)(2,1)}), bf16[16,4,2,8,512]{4,3,2,1,0:T(8,128)(2,1)S(1)}, u32[]{:S(2)}, u32[]{:S(2)}) async-start(bf16[16,4,2,8,512]{4,3,2,1,0:T(8,128)(2,1)} %broadcast_in_dim.44), calls=%async_computation | async-start | bytes 2097152 | tf_op jit(solution)/shard_map/all_to_all | solution.py:151
  40.1 0.6 fusion.34
  40.7 0.6 fusion.38
  41.3 0.6 fusion.37
  42.0 0.0 copy-done.5
  42.0 0.6 fusion.36
  42.6 0.1 copy.54
  42.7 0.0 copy-start.1
  42.7 1.9 %collective-permute-start.2 = (bf16[4,256,512]{2,1,0:T(8,128)(2,1)S(1)}, bf16[4,256,512]{2,1,0:T(8,128)(2,1)}, u32[]{:S(2)}, u32[]{:S(2)}) collective-permute-start(bf16[4,256,512]{2,1,0:T(8,128)(2,1)S(1)} %bitcast.77), channel_id=1, source_target_pairs={{0,8},{8,0},{1,9},{9,1},{2,10},{10,2},{3,11},{11,3},{4,12},{12,4},... | collective-permute-start | bytes 3145736 | tf_op jit(solution)/shard_map/ppermute | solution.py:153
  44.7 10.8 %all-to-all-done = bf16[16,4,2,8,512]{4,3,2,1,0:T(8,128)(2,1)S(1)} async-done(((bf16[16,4,2,8,512]{4,3,2,1,0:T(8,128)(2,1)}), bf16[16,4,2,8,512]{4,3,2,1,0:T(8,128)(2,1)S(1)}, u32[]{:S(2)}, u32[]{:S(2)}) %all-to-all-start) | async-done | bytes 1048608 | tf_op jit(solution)/shard_map/all_to_all | solution.py:151
  55.5 0.1 copy.53
  55.6 0.0 copy-start.2
  55.6 1.9 %collective-permute-start.1 = (bf16[4,256,512]{2,1,0:T(8,128)(2,1)S(1)}, bf16[4,256,512]{2,1,0:T(8,128)(2,1)S(1)}, u32[]{:S(2)}, u32[]{:S(2)}) collective-permute-start(bf16[4,256,512]{2,1,0:T(8,128)(2,1)S(1)} %bitcast.79), channel_id=1, source_target_pairs={{0,8},{8,0},{1,9},{9,1},{2,10},{10,2},{3,11},{11,3},{4,12},{12,4},... | collective-permute-start | bytes 3145736 | tf_op jit(solution)/shard_map/ppermute | solution.py:153
  57.5 0.6 fusion.35
  58.1 0.1 stack_reshape.3
  58.3 0.0 copy-done.1
  58.3 1.6 %copy.48 = bf16[4,5,8,512]{3,2,1,0:T(8,128)(2,1)} copy(bf16[4,5,8,512]{3,0,2,1:T(4,128)(2,1)} %bitcast.7) | data formatting | bytes 327680 | tf_op jit(solution)/shard_map/convert_element_type | solution.py:190
  59.9 0.0 copy-done.7
  59.9 0.6 reduce_precision.3.table
  60.5 0.1 pad_add_fusion
  60.6 0.7 pad_maximum_fusion
  61.3 2.0 %convolution_convert_fusion = s32[160,512]{1,0:T(8,128)} fusion(bf16[160,512]{1,0:T(8,128)(2,1)} %bitcast.89, s32[512]{0:T(512)S(1)} %fusion.48), kind=kOutput, calls=%fused_computation.2 | convolution fusion | flops 84230144 | bytes 493568 | tf_op jit(solution)/shard_map/dot_general | solution.py:189
  63.3 0.0 collective-permute-done.2.far
  63.3 0.7 broadcast_in_dim.43.urow
  64.0 1.1 broadcast_8_send_in_keep_in.2.send_in
  65.1 0.0 copy-done.2
  65.1 1.1 broadcast_8_send_in_keep_in.2.clone.keep_in
  66.2 18.7 %shard_map.73 = (f32[384,768]{1,0:T(8,128)}, f32[384,768]{1,0:T(8,128)}) custom-call(f32[8,7]{1,0:T(8,128)} %reduce_precision.3.table, s32[4,5,8,512]{3,2,1,0:T(8,128)} %bitcast.82, s32[96,256]{1,0:T(8,128)} %broadcast_in_dim.43.urow, bf16[4,32,512]{2,1,0:T(8,128)(2,1)} %bitcast.84, ...), custom_call_target="tpu_custom_call", output_to_operand_aliasing={{0}: (6, {}), {1}: (7, {})} | custom-call | tf_op jit(solution)/shard_map/pallas_call | solution.py:124
  85.0 0.0 collective-permute-done.1.far
  85.0 0.0 copy-start.3
  85.0 1.0 copy-done.3
  85.9 18.7 %shard_map.74 = (f32[384,768]{1,0:T(8,128)}, f32[384,768]{1,0:T(8,128)}) custom-call(f32[8,7]{1,0:T(8,128)} %reduce_precision.3.table, s32[4,5,8,512]{3,2,1,0:T(8,128)} %bitcast.83, s32[96,256]{1,0:T(8,128)} %broadcast_in_dim.43.urow, bf16[4,32,512]{2,1,0:T(8,128)(2,1)} %bitcast.85, ...), custom_call_target="tpu_custom_call", output_to_operand_aliasing={{0}: (6, {}), {1}: (7, {})} | custom-call | tf_op jit(solution)/shard_map/pallas_call | solution.py:124
  104.6 1.4 convert_element_type.49
  106.1 2.4 %collective-permute-start.3 = (bf16[384,768]{1,0:T(8,128)(2,1)S(1)}, bf16[384,768]{1,0:T(8,128)(2,1)S(1)}, u32[]{:S(2)}, u32[]{:S(2)}) collective-permute-start(bf16[384,768]{1,0:T(8,128)(2,1)S(1)} %convert_element_type.49), channel_id=1, source_target_pairs={{0,8},{8,0},{1,9},{9,1},{2,10},{10,2},{3,11},{11,3},{4,12},{12,4},... | collective-permute-start | bytes 1769480 | tf_op jit(solution)/shard_map/ppermute | solution.py:205
  108.5 1.6 %collective-permute-done.3 = bf16[384,768]{1,0:T(8,128)(2,1)S(1)} collective-permute-done((bf16[384,768]{1,0:T(8,128)(2,1)S(1)}, bf16[384,768]{1,0:T(8,128)(2,1)S(1)}, u32[]{:S(2)}, u32[]{:S(2)}) %collective-permute-start.3) | collective-permute-done | bytes 589856 | tf_op jit(solution)/shard_map/ppermute | solution.py:205
  110.1 0.1 add_convert_fusion
  110.2 16.1 %all_to_all.20 = bf16[16,24,768]{2,1,0:T(8,128)(2,1)S(1)} all-to-all(bf16[16,24,768]{2,1,0:T(8,128)(2,1)S(1)} %bitcast.81), channel_id=1, replica_groups=mesh['x'=4,'y'=4,'zh'=2,'core'=2,'chan'=8] {'x','y'}, dimensions={0} | all-to-all | bytes 1179648 | tf_op jit(solution)/shard_map/all_to_all | solution.py:207
  126.4 0.1 convert_reduce_fusion
  126.4 0.1 reshape.175
  126.6 26.4 %all_to_all.21 = f32[16,12,96]{2,1,0:T(8,128)S(1)} all-to-all(f32[16,12,96]{2,1,0:T(8,128)S(1)} %copy.56), channel_id=1, replica_groups=mesh['x'=4,'y'=4,'zh'=2,'core'=2,'chan'=8] {'zh','chan'}, dimensions={0} | all-to-all | bytes 147456 | tf_op jit(solution)/shard_map/all_to_all | solution.py:210
  153.1 0.1 reshape.177
  153.2 0.6 copy.57
  (19 shorter events, 0.2 us)
Async XLA Ops:
  7.1 22.0 %copy-start.6 = (s32[1,8,4,512,1]{3,4,2,1,0:T(1,128)S(1)}, s32[1,8,4,512,1]{3,4,2,1,0:T(1,128)}, u32[]{:S(2)}) copy-start(s32[1,8,4,512,1]{3,4,2,1,0:T(1,128)} %param.10) | copy-start | bytes 196612
  7.1 22.2 %copy-start.4 = (s32[1,8,4,512,2]{3,4,2,1,0:T(2,128)S(1)}, s32[1,8,4,512,2]{3,4,2,1,0:T(2,128)}, u32[]{:S(2)}) copy-start(s32[1,8,4,512,2]{3,4,2,1,0:T(2,128)} %param.11) | copy-start | bytes 393220
  7.1 22.2 %copy-start.8 = (s32[32]{0:T(128)S(1)}, s32[32]{0:T(128)}, u32[]{:S(2)}) copy-start(s32[32]{0:T(128)} %param.13) | copy-start | bytes 388
  7.1 25.5 %all-to-all-start.1 = ((bf16[16,4,2,8,512]{4,3,2,1,0:T(8,128)(2,1)}), bf16[16,4,2,8,512]{4,3,2,1,0:T(8,128)(2,1)S(1)}, u32[]{:S(2)}, u32[]{:S(2)}) async-start(bf16[16,4,2,8,512]{4,3,2,1,0:T(8,128)(2,1)} %broadcast_in_dim.45), calls=%async_computation.1 | async-start | bytes 2097152 | tf_op jit(solution)/shard_map/all_to_all | solution.py:151
  14.2 18.3 %collective-permute-start = (bf16[4,2,8,512]{3,2,1,0:T(8,128)(2,1)S(1)}, bf16[4,2,8,512]{3,2,1,0:T(8,128)(2,1)S(1)}, u32[]{:S(2)}, u32[]{:S(2)}) collective-permute-start(bf16[4,2,8,512]{3,2,1,0:T(8,128)(2,1)S(1)} %reshape.170), channel_id=1, source_target_pairs={{0,16},{16,0},{1,17},{17,1},{2,18},{18,2},{3,19},{19,3},{4,20},{20... | collective-permute-start | bytes 196616 | tf_op jit(solution)/shard_map/ppermute | solution.py:168
  33.7 8.3 %copy-start.5 = (s32[1,8,4,512,2]{3,4,2,1,0:T(2,128)S(1)}, s32[1,8,4,512,2]{3,4,2,1,0:T(2,128)}, u32[]{:S(2)}) copy-start(s32[1,8,4,512,2]{3,4,2,1,0:T(2,128)} %param.12) | copy-start | bytes 393220
  33.7 21.7 %all-to-all-start = ((bf16[16,4,2,8,512]{4,3,2,1,0:T(8,128)(2,1)}), bf16[16,4,2,8,512]{4,3,2,1,0:T(8,128)(2,1)S(1)}, u32[]{:S(2)}, u32[]{:S(2)}) async-start(bf16[16,4,2,8,512]{4,3,2,1,0:T(8,128)(2,1)} %broadcast_in_dim.44), calls=%async_computation | async-start | bytes 2097152 | tf_op jit(solution)/shard_map/all_to_all | solution.py:151
  42.7 15.5 %copy-start.1 = (bf16[4,2,16,8,512]{4,3,2,1,0:T(8,128)(2,1)}, bf16[4,2,16,8,512]{4,3,2,1,0:T(8,128)(2,1)S(1)}, u32[]{:S(2)}) copy-start(bf16[4,2,16,8,512]{4,3,2,1,0:T(8,128)(2,1)S(1)} %copy.54) | copy-start | bytes 3145732
  42.7 20.6 %collective-permute-start.2 = (bf16[4,256,512]{2,1,0:T(8,128)(2,1)S(1)}, bf16[4,256,512]{2,1,0:T(8,128)(2,1)}, u32[]{:S(2)}, u32[]{:S(2)}) collective-permute-start(bf16[4,256,512]{2,1,0:T(8,128)(2,1)S(1)} %bitcast.77), channel_id=1, source_target_pairs={{0,8},{8,0},{1,9},{9,1},{2,10},{10,2},{3,11},{11,3},{4,12},{12,4},... | collective-permute-start | bytes 3145736 | tf_op jit(solution)/shard_map/ppermute | solution.py:153
  55.5 4.4 %copy-start.7 = (f32[8,7]{1,0:T(8,128)S(1)}, f32[8,7]{1,0:T(8,128)}, u32[]{:S(2)}) copy-start(f32[8,7]{1,0:T(8,128)} %param.9) | copy-start | bytes 676
  55.6 9.6 %copy-start.2 = (bf16[4,2,16,8,512]{4,3,2,1,0:T(8,128)(2,1)}, bf16[4,2,16,8,512]{4,3,2,1,0:T(8,128)(2,1)S(1)}, u32[]{:S(2)}) copy-start(bf16[4,2,16,8,512]{4,3,2,1,0:T(8,128)(2,1)S(1)} %copy.53) | copy-start | bytes 3145732
  55.6 29.4 %collective-permute-start.1 = (bf16[4,256,512]{2,1,0:T(8,128)(2,1)S(1)}, bf16[4,256,512]{2,1,0:T(8,128)(2,1)S(1)}, u32[]{:S(2)}, u32[]{:S(2)}) collective-permute-start(bf16[4,256,512]{2,1,0:T(8,128)(2,1)S(1)} %bitcast.79), channel_id=1, source_target_pairs={{0,8},{8,0},{1,9},{9,1},{2,10},{10,2},{3,11},{11,3},{4,12},{12,4},... | collective-permute-start | bytes 3145736 | tf_op jit(solution)/shard_map/ppermute | solution.py:153
  85.0 1.0 copy-start.3
  104.6 5.5 %copy-start = (f32[384,768]{1,0:T(8,128)S(1)}, f32[384,768]{1,0:T(8,128)}, u32[]{:S(2)}) copy-start(f32[384,768]{1,0:T(8,128)} %get-tuple-element.11) | copy-start | bytes 3538948
  106.1 4.0 %collective-permute-start.3 = (bf16[384,768]{1,0:T(8,128)(2,1)S(1)}, bf16[384,768]{1,0:T(8,128)(2,1)S(1)}, u32[]{:S(2)}, u32[]{:S(2)}) collective-permute-start(bf16[384,768]{1,0:T(8,128)(2,1)S(1)} %convert_element_type.49), channel_id=1, source_target_pairs={{0,8},{8,0},{1,9},{9,1},{2,10},{10,2},{3,11},{11,3},{4,12},{12,4},... | collective-permute-start | bytes 1769480 | tf_op jit(solution)/shard_map/ppermute | solution.py:205

commit v3 on v2

--- a/solution.py
+++ b/solution.py
@@ -2,6 +2,7 @@
 
 import jax
 import jax.numpy as jnp
+import numpy as np
 from jax import lax
 from jax.experimental import pallas as pl
 from jax.experimental.pallas import tpu as pltpu
@@ -19,20 +20,19 @@
 KW = 7
 OS = 8
 SIDE = 768
-PART = 256
-BUNCH = 2
+PART = 128
+BUNCH = 4
 STN = ("x", "y", "zh", "core")
 
 
 def fourier_table(length):
-    index = jnp.arange(length, dtype=jnp.int32)
-    phase = index[:, None] * index[None, :] % length
-    angle = phase.astype(jnp.float32) * (2.0 * math.pi / length)
-    cosine = jnp.cos(angle) / math.sqrt(length)
-    sine = jnp.sin(angle) / math.sqrt(length)
-    upper = jnp.concatenate([cosine, -sine], axis=1)
-    lower = jnp.concatenate([sine, cosine], axis=1)
-    return jnp.concatenate([upper, lower], axis=0)
+    index = np.arange(length)
+    angle = (index[:, None] * index[None, :] % length) * (2.0 * math.pi / length)
+    cosine = np.cos(angle) / math.sqrt(length)
+    sine = np.sin(angle) / math.sqrt(length)
+    upper = np.concatenate([cosine, -sine], axis=1)
+    lower = np.concatenate([sine, cosine], axis=1)
+    return np.concatenate([upper, lower], axis=0).astype(np.float32)
 
 
 def channelize(voltages, prototype):
@@ -51,26 +51,20 @@
     return spectra.transpose(4, 1, 0, 3, 2, 5).reshape(CT, 2, stations, 2 * FRAMES * CB)
 
 
-def grid_body(
-    table, index, urow, lhs, near, far, send_in, keep_in, send, keep, vis, taps, amat, wmat
-):
+def grid_body(table, index, urow, lhs, rhs, *rest):
+    earlier, (send, keep, vis, taps, amat, wmat) = rest[:-6], rest[-6:]
     step = pl.program_id(0)
 
     @pl.when(step == 0)
     def _():
-        send[...] = send_in[...]
-        keep[...] = keep_in[...]
-
-    width = PART // 2
-    for side, rhs in enumerate((near, far)):
-        product = lax.dot_general(
-            lhs[0], rhs[0], (((1,), (1,)), ((), ())), preferred_element_type=jnp.float32
-        )
-        product = (product * (1.0 / (FRAMES * CB))).astype(jnp.bfloat16).astype(jnp.float32)
-        product = product.reshape(4, STN_DEV, 2 * width)
-        for q in range(2):
-            first = q * PART + side * width
-            vis[:, :, first : first + width] = product[:, :, q * width : (q + 1) * width]
+        send[...] = earlier[0][...] if earlier else jnp.zeros_like(send)
+        keep[...] = earlier[1][...] if earlier else jnp.zeros_like(keep)
+
+    product = lax.dot_general(
+        lhs[0], rhs[0], (((1,), (1,)), ((), ())), preferred_element_type=jnp.float32
+    )
+    product = (product * (1.0 / (FRAMES * CB))).astype(jnp.bfloat16).astype(jnp.float32)
+    vis[...] = product.reshape(4, STN_DEV, 2 * PART)
     for axis in range(2):
         chosen = index[0, 3 + axis]
         masks = [chosen == o for o in range(1, OS)]
@@ -82,30 +76,37 @@
 
     def stations(turn, carry):
         for inner in range(BUNCH):
-            row = pl.ds(turn * BUNCH + inner, 1)
+            def pick(ref, lead, lanes=slice(None)):
+                low = ref[lead + (slice(inner, inner + 1), lanes)]
+                up = ref[lead + (slice(BUNCH + inner, BUNCH + inner + 1), lanes)]
+                return jnp.where(turn == 0, low, up)
+
             lanes = slice(inner * PART, (inner + 1) * PART)
-            position = index[0, 0, row, :]
-            u0 = index[0, 1, row, :] + 64 * (position & 1) - KW // 2
-            v0 = index[0, 2, row, :] - KW // 2
+            position = pick(index, (0, 0))
+            u0 = pick(index, (0, 1)) + 64 * (position & 1) - KW // 2
+            v0 = pick(index, (0, 2)) - KW // 2
             high = position >> 1
             shape = (G, PART)
             away = lax.broadcasted_iota(jnp.int32, shape, 0) - v0
             down = jnp.zeros(shape, jnp.float32)
             for k in range(KW):
-                down = jnp.where(away == k, taps[KW + k, row, :], down)
+                down = jnp.where(away == k, pick(taps, (KW + k,)), down)
             for h in range(NSUB // 2):
                 amat[h * G : (h + 1) * G, lanes] = jnp.where(high == h, down, 0.0).astype(
                     jnp.bfloat16
                 )
+            tap_rows = [pick(taps, (k,)) for k in range(KW)]
+            values = [
+                pick(vis, (j // 2,), slice((j % 2) * PART, (j % 2 + 1) * PART)) for j in range(8)
+            ]
             for half in range(2):
                 away = urow[half * G : (half + 1) * G, :] - u0
                 across = jnp.zeros(shape, jnp.float32)
                 for k in range(KW):
-                    across = jnp.where(away == k, taps[k, row, :], across)
+                    across = jnp.where(away == k, tap_rows[k], across)
                 for j in range(8):
-                    value = vis[j // 2, row, (j % 2) * PART : (j % 2 + 1) * PART]
                     first = half * 8 * G + j * G
-                    wmat[first : first + G, lanes] = (value * across).astype(jnp.bfloat16)
+                    wmat[first : first + G, lanes] = (values[j] * across).astype(jnp.bfloat16)
         total = lax.dot_general(
             wmat[...], amat[...], (((1,), (1,)), ((), ())), preferred_element_type=jnp.float32
         )
@@ -116,11 +117,10 @@
     lax.fori_loop(0, STN_DEV // BUNCH, stations, 0)
 
 
-def grid_tiles(table, index, urow, lhs, near, far, send, keep, part):
+def grid_tiles(table, index, urow, lhs, rhs, earlier, part):
     half = jax.ShapeDtypeStruct((SIDE // 2, SIDE), jnp.float32)
     whole = pl.BlockSpec((SIDE // 2, SIDE), lambda t: (0, 0))
     lanes = 2 * FRAMES * CB
-    piece = pl.BlockSpec((1, PART, lanes), lambda t: (t, 0, 0))
     return pl.pallas_call(
         grid_body,
         grid=(CT,),
@@ -129,28 +129,27 @@
             pl.BlockSpec((1, 5, STN_DEV, PART), lambda t: (t, 0, 0, part)),
             pl.BlockSpec((2 * G, PART), lambda t: (0, 0)),
             pl.BlockSpec((1, 4 * STN_DEV, lanes), lambda t: (t, 0, 0)),
-            piece,
-            piece,
-            whole,
-            whole,
-        ],
+            pl.BlockSpec((1, 2 * PART, lanes), lambda t: (t, 0, 0)),
+        ]
+        + [whole] * len(earlier),
         out_specs=[whole, whole],
         out_shape=[half, half],
-        input_output_aliases={6: 0, 7: 1},
+        input_output_aliases={5: 0, 6: 1} if earlier else {},
         scratch_shapes=[
             pltpu.VMEM((4, STN_DEV, 2 * PART), jnp.float32),
             pltpu.VMEM((2 * KW, STN_DEV, PART), jnp.float32),
             pltpu.VMEM((SIDE, BUNCH * PART), jnp.bfloat16),
             pltpu.VMEM((SIDE, BUNCH * PART), jnp.bfloat16),
         ],
-    )(table, index, urow, lhs, near, far, send, keep)
+    )(table, index, urow, lhs, rhs, *earlier)
 
 
 def spread_over_plane(spectra):
     copies = jnp.broadcast_to(spectra, (16,) + spectra.shape)
     pieces = lax.all_to_all(copies, ("x", "y"), 0, 0, tiled=True)
-    near = pieces.transpose(1, 2, 0, 3, 4).reshape(CT, PART, 2 * FRAMES * CB)
-    return near, lax.ppermute(near, "core", [(0, 1), (1, 0)])
+    near = pieces.transpose(1, 2, 0, 3, 4).reshape(CT, 2 * PART, 2 * FRAMES * CB)
+    far = lax.ppermute(near, "core", [(0, 1), (1, 0)])
+    return [near, far]
 
 
 def arrival_order():
@@ -160,13 +159,13 @@
     return ((slot // 8 % 16) * 4 + zh * 2 + core) * STN_DEV + slot % 8
 
 
-def per_device(
+def whole_step(
     voltages, prototype, kernel_table, tile_subgrid, tile_cells, tile_offsets, subgrid_slot
 ):
     swap = [(0, 1), (1, 0)]
     spectra = channelize(voltages, prototype)
     other = lax.ppermute(spectra, "zh", swap)
-    parts = (spread_over_plane(spectra), spread_over_plane(other))
+    parts = spread_over_plane(spectra)
     lanes = FRAMES * CB
     turned = jnp.concatenate([spectra[..., lanes:], -spectra[..., :lanes]], axis=-1)
     lhs = jnp.stack([spectra, turned], axis=1).reshape(CT, 4 * STN_DEV, 2 * lanes)
@@ -198,10 +197,12 @@
     urow = jnp.broadcast_to(urow[:, None], (2 * G, PART))
     table = lax.reduce_precision(kernel_table, 8, 7)
 
-    send = jnp.zeros((SIDE // 2, SIDE), jnp.float32)
-    keep = jnp.zeros((SIDE // 2, SIDE), jnp.float32)
-    for part, (near, far) in enumerate(parts):
-        send, keep = grid_tiles(table, index, urow, lhs, near, far, send, keep, part)
+    other, table, index, urow, lhs = lax.optimization_barrier((other, table, index, urow, lhs))
+    parts = parts + spread_over_plane(other)
+    grids = ()
+    for part, rhs in enumerate(parts):
+        grids = grid_tiles(table, index, urow, lhs, rhs, grids, part)
+    send, keep = grids
     total = keep + lax.ppermute(send.astype(jnp.bfloat16), "core", swap).astype(jnp.float32)
     total = total.astype(jnp.bfloat16).reshape(16, 24, SIDE)
     total = lax.all_to_all(total, ("x", "y"), 0, 0, tiled=True)
@@ -215,7 +216,7 @@
 def solution(mesh):
     fine = Mesh(mesh.devices.reshape(4, 4, 2, 2, 8), STN + ("chan",))
     return jax.shard_map(
-        per_device,
+        whole_step,
         mesh=fine,
         in_specs=(
             P(STN, None, None, "chan", None),

time: 155 us -> 162 us (1.045)
  the two profiles are of different devices: /device:TPU:32 before, /device:TPU:2 now
where the time goes in v3:
time: 162 us; the launch traced here: 161 us
  Pallas kernels  51.9 us (32%)
  blocking collectives  35.7 us (22%)
  starting transfers between devices  35.6 us (22%)
  waiting for transfers between devices  23.4 us (14%)
  local copies, waits for them, and re-layouts  8.38 us (5%)
  other arithmetic  4.27 us (3%)
  matrix products  1.84 us (1%)
    pallas_call x4, Pallas kernels, grid_tiles(): pl.pallas_call(grid_body, grid=(CT,), in_specs=[pl.BlockSpec(memory_space...  51.9 us
    all_to_all x2, waiting for transfers between devices, spread_over_plane(): pieces = lax.all_to_all(copies, ('x', 'y'), 0, 0, tiled=True)  21.8 us
    all_to_all x1, blocking collectives, whole_step(): lax.all_to_all(total, ('zh', 'chan'), 0, 0, tiled=True)  19 us
    all_to_all x1, blocking collectives, whole_step(): total = lax.all_to_all(total, ('x', 'y'), 0, 0, tiled=True)  16.6 us
    ppermute x1, starting transfers between devices, whole_step(): other = lax.ppermute(spectra, 'zh', swap)  15.7 us
    all_to_all x2, starting transfers between devices, spread_over_plane(): pieces = lax.all_to_all(copies, ('x', 'y'), 0, 0, tiled=True)  13.6 us
    ppermute x2, starting transfers between devices, spread_over_plane(): far = lax.ppermute(near, 'core', [(0, 1), (1, 0)])  3.84 us
  transfers between devices with their start and end apart: 6, of which 3 were waited for; matrix products, arithmetic and copies ran while one was open for 3% of the time, Pallas kernels for 24%

profile of v3, /device:TPU:2, one launch (start us, length us, event | category | flops | bytes accessed | tf_op | source)
XLA Modules:
  0.0 161.4 jit_solution(11551083165775720620)
XLA Ops:
  0.0 1.0 fusion.55
  1.0 1.0 copy.47
  2.1 0.1 reshape.179
  2.2 0.0 copy-start.4
  2.2 0.5 fusion.2
  2.7 0.1 copy.48
  2.8 0.6 copy-done.4
  3.4 0.8 convolution_convert_fusion.1
  4.2 0.1 reshape.166
  4.3 0.1 copy.49
  4.4 0.1 reshape.167
  4.5 15.7 %collective-permute-start = (bf16[4,2,8,512]{3,2,1,0:T(8,128)(2,1)S(1)}, bf16[4,2,8,512]{3,2,1,0:T(8,128)(2,1)S(1)}, u32[]{:S(2)}, u32[]{:S(2)}) collective-permute-start(bf16[4,2,8,512]{3,2,1,0:T(8,128)(2,1)S(1)} %reshape.167), channel_id=1, source_target_pairs={{0,16},{16,0},{1,17},{17,1},{2,18},{18,2},{3,19},{19,3},{4,20},{20... | collective-permute-start | bytes 196616 | tf_op jit(solution)/shard_map/ppermute | solution.py:167
  20.2 1.1 broadcast_in_dim.43
  21.3 0.0 copy-start.7
  21.3 0.0 copy-start.5
  21.3 0.0 copy-start.9
  21.3 0.0 copy-start.6
  21.3 7.6 %all-to-all-start.1 = ((bf16[16,4,2,8,512]{4,3,2,1,0:T(8,128)(2,1)}), bf16[16,4,2,8,512]{4,3,2,1,0:T(8,128)(2,1)S(1)}, u32[]{:S(2)}, u32[]{:S(2)}) async-start(bf16[16,4,2,8,512]{4,3,2,1,0:T(8,128)(2,1)} %broadcast_in_dim.43), calls=%async_computation.1 | async-start | bytes 2097152 | tf_op jit(solution)/shard_map/all_to_all | solution.py:149
  29.0 0.0 copy-start.8
  29.0 0.1 stack_reshape.3
  29.1 0.1 iota_compare_fusion.3
  29.2 0.0 copy-done.7
  29.2 0.0 copy-done.5
  29.3 0.0 copy-done.9
  29.3 0.5 select_reduce_fusion
  29.9 0.0 copy-done.6
  30.1 0.0 copy-done.8
  30.1 0.6 reduce_precision.3.table
  30.7 0.7 pad_maximum_fusion
  31.4 1.1 convolution_convert_fusion
  32.5 0.1 pad_add_fusion
  32.6 0.0 collective-permute-done
  32.6 0.7 broadcast_in_dim.41.urow
  33.3 10.5 %all-to-all-done.1 = bf16[16,4,2,8,512]{4,3,2,1,0:T(8,128)(2,1)S(1)} async-done(((bf16[16,4,2,8,512]{4,3,2,1,0:T(8,128)(2,1)}), bf16[16,4,2,8,512]{4,3,2,1,0:T(8,128)(2,1)S(1)}, u32[]{:S(2)}, u32[]{:S(2)}) %all-to-all-start.1) | async-done | bytes 1048608 | tf_op jit(solution)/shard_map/all_to_all | solution.py:149
  43.8 1.1 broadcast_in_dim.42
  44.9 6.0 %all-to-all-start = ((bf16[16,4,2,8,512]{4,3,2,1,0:T(8,128)(2,1)}), bf16[16,4,2,8,512]{4,3,2,1,0:T(8,128)(2,1)S(1)}, u32[]{:S(2)}, u32[]{:S(2)}) async-start(bf16[16,4,2,8,512]{4,3,2,1,0:T(8,128)(2,1)} %broadcast_in_dim.42), calls=%async_computation | async-start | bytes 2097152 | tf_op jit(solution)/shard_map/all_to_all | solution.py:149
  51.0 0.1 copy.57
  51.1 0.0 copy-start.2
  51.1 1.9 %collective-permute-start.2 = (bf16[4,256,512]{2,1,0:T(8,128)(2,1)S(1)}, bf16[4,256,512]{2,1,0:T(8,128)(2,1)}, u32[]{:S(2)}, u32[]{:S(2)}) collective-permute-start(bf16[4,256,512]{2,1,0:T(8,128)(2,1)S(1)} %bitcast.83), channel_id=1, source_target_pairs={{0,8},{8,0},{1,9},{9,1},{2,10},{10,2},{3,11},{11,3},{4,12},{12,4},... | collective-permute-start | bytes 3145736 | tf_op jit(solution)/shard_map/ppermute | solution.py:151
  53.0 11.3 %all-to-all-done = bf16[16,4,2,8,512]{4,3,2,1,0:T(8,128)(2,1)S(1)} async-done(((bf16[16,4,2,8,512]{4,3,2,1,0:T(8,128)(2,1)}), bf16[16,4,2,8,512]{4,3,2,1,0:T(8,128)(2,1)S(1)}, u32[]{:S(2)}, u32[]{:S(2)}) %all-to-all-start) | async-done | bytes 1048608 | tf_op jit(solution)/shard_map/all_to_all | solution.py:149
  64.3 0.1 copy.56
  64.4 0.0 copy-start.1
  64.4 1.9 %collective-permute-start.1 = (bf16[4,256,512]{2,1,0:T(8,128)(2,1)S(1)}, bf16[4,256,512]{2,1,0:T(8,128)(2,1)S(1)}, u32[]{:S(2)}, u32[]{:S(2)}) collective-permute-start(bf16[4,256,512]{2,1,0:T(8,128)(2,1)S(1)} %bitcast.80), channel_id=1, source_target_pairs={{0,8},{8,0},{1,9},{9,1},{2,10},{10,2},{3,11},{11,3},{4,12},{12,4},... | collective-permute-start | bytes 3145736 | tf_op jit(solution)/shard_map/ppermute | solution.py:151
  66.3 0.0 copy-done.2
  66.3 12.4 %shard_map.82 = (f32[384,768]{1,0:T(8,128)}, f32[384,768]{1,0:T(8,128)}) custom-call(f32[8,7]{1,0:T(8,128)} %reduce_precision.3.table, s32[4,5,8,512]{3,2,1,0:T(8,128)} %bitcast.76, s32[96,128]{1,0:T(8,128)} %broadcast_in_dim.41.urow, bf16[4,32,512]{2,1,0:T(8,128)(2,1)} %bitcast.86, bf16[4,256,512]{2,1,0:T(8,128)(2,1)} %bitcast.84), custom_call_target="tpu_custom_call" | custom-call | tf_op jit(solution)/shard_map/pallas_call | solution.py:124
  78.7 0.0 collective-permute-done.2.rhs
  78.7 13.2 %shard_map.83 = (f32[384,768]{1,0:T(8,128)}, f32[384,768]{1,0:T(8,128)}) custom-call(f32[8,7]{1,0:T(8,128)} %reduce_precision.3.table, s32[4,5,8,512]{3,2,1,0:T(8,128)} %bitcast.77, s32[96,128]{1,0:T(8,128)} %broadcast_in_dim.41.urow, bf16[4,32,512]{2,1,0:T(8,128)(2,1)} %bitcast.87, ...), custom_call_target="tpu_custom_call", output_to_operand_aliasing={{0}: (5, {}), {1}: (6, {})} | custom-call | tf_op jit(solution)/shard_map/pallas_call | solution.py:124
  91.9 0.0 copy-done.1
  91.9 13.2 %shard_map.84 = (f32[384,768]{1,0:T(8,128)}, f32[384,768]{1,0:T(8,128)}) custom-call(f32[8,7]{1,0:T(8,128)} %reduce_precision.3.table, s32[4,5,8,512]{3,2,1,0:T(8,128)} %bitcast.78, s32[96,128]{1,0:T(8,128)} %broadcast_in_dim.41.urow, bf16[4,32,512]{2,1,0:T(8,128)(2,1)} %bitcast.88, ...), custom_call_target="tpu_custom_call", output_to_operand_aliasing={{0}: (5, {}), {1}: (6, {})} | custom-call | tf_op jit(solution)/shard_map/pallas_call | solution.py:124
  105.1 0.0 collective-permute-done.1.rhs
  105.1 0.0 copy-start.3
  105.1 1.0 copy-done.3
  106.0 13.2 %shard_map.85 = (f32[384,768]{1,0:T(8,128)}, f32[384,768]{1,0:T(8,128)}) custom-call(f32[8,7]{1,0:T(8,128)} %reduce_precision.3.table, s32[4,5,8,512]{3,2,1,0:T(8,128)} %bitcast.79, s32[96,128]{1,0:T(8,128)} %broadcast_in_dim.41.urow, bf16[4,32,512]{2,1,0:T(8,128)(2,1)} %bitcast.89, ...), custom_call_target="tpu_custom_call", output_to_operand_aliasing={{0}: (5, {}), {1}: (6, {})} | custom-call | tf_op jit(solution)/shard_map/pallas_call | solution.py:124
  119.2 1.4 convert_element_type.39
  120.6 2.4 %collective-permute-start.3 = (bf16[384,768]{1,0:T(8,128)(2,1)S(1)}, bf16[384,768]{1,0:T(8,128)(2,1)S(1)}, u32[]{:S(2)}, u32[]{:S(2)}) collective-permute-start(bf16[384,768]{1,0:T(8,128)(2,1)S(1)} %convert_element_type.39), channel_id=1, source_target_pairs={{0,8},{8,0},{1,9},{9,1},{2,10},{10,2},{3,11},{11,3},{4,12},{12,4},... | collective-permute-start | bytes 1769480 | tf_op jit(solution)/shard_map/ppermute | solution.py:206
  123.0 1.6 collective-permute-done.3
  124.7 0.0 copy-done
  124.7 0.1 add_convert_fusion
  124.8 16.6 %all_to_all.20 = bf16[16,24,768]{2,1,0:T(8,128)(2,1)S(1)} all-to-all(bf16[16,24,768]{2,1,0:T(8,128)(2,1)S(1)} %bitcast.90), channel_id=1, replica_groups=mesh['x'=4,'y'=4,'zh'=2,'core'=2,'chan'=8] {'x','y'}, dimensions={0} | all-to-all | bytes 1179648 | tf_op jit(solution)/shard_map/all_to_all | solution.py:208
  141.4 0.1 convert_reduce_fusion
  141.5 0.1 reshape.175
  141.6 19.0 %all_to_all.21 = f32[16,12,96]{2,1,0:T(8,128)S(1)} all-to-all(f32[16,12,96]{2,1,0:T(8,128)S(1)} %copy.59), channel_id=1, replica_groups=mesh['x'=4,'y'=4,'zh'=2,'core'=2,'chan'=8] {'zh','chan'}, dimensions={0} | all-to-all | bytes 147456 | tf_op jit(solution)/shard_map/all_to_all | solution.py:211
  160.7 0.1 reshape.177
  160.8 0.6 copy.60
  (19 shorter events, 0.4 us)
Async XLA Ops:
  2.2 1.2 copy-start.4
  4.5 28.1 %collective-permute-start = (bf16[4,2,8,512]{3,2,1,0:T(8,128)(2,1)S(1)}, bf16[4,2,8,512]{3,2,1,0:T(8,128)(2,1)S(1)}, u32[]{:S(2)}, u32[]{:S(2)}) collective-permute-start(bf16[4,2,8,512]{3,2,1,0:T(8,128)(2,1)S(1)} %reshape.167), channel_id=1, source_target_pairs={{0,16},{16,0},{1,17},{17,1},{2,18},{18,2},{3,19},{19,3},{4,20},{20... | collective-permute-start | bytes 196616 | tf_op jit(solution)/shard_map/ppermute | solution.py:167
  21.3 7.9 %copy-start.7 = (s32[1,8,4,512,1]{3,4,2,1,0:T(1,128)S(1)}, s32[1,8,4,512,1]{3,4,2,1,0:T(1,128)}, u32[]{:S(2)}) copy-start(s32[1,8,4,512,1]{3,4,2,1,0:T(1,128)} %param.11) | copy-start | bytes 196612
  21.3 7.9 %copy-start.5 = (s32[1,8,4,512,2]{3,4,2,1,0:T(2,128)S(1)}, s32[1,8,4,512,2]{3,4,2,1,0:T(2,128)}, u32[]{:S(2)}) copy-start(s32[1,8,4,512,2]{3,4,2,1,0:T(2,128)} %param.12) | copy-start | bytes 393220
  21.3 8.0 %copy-start.9 = (s32[32]{0:T(128)S(1)}, s32[32]{0:T(128)}, u32[]{:S(2)}) copy-start(s32[32]{0:T(128)} %param.14) | copy-start | bytes 388
  21.3 8.6 %copy-start.6 = (s32[1,8,4,512,2]{3,4,2,1,0:T(2,128)S(1)}, s32[1,8,4,512,2]{3,4,2,1,0:T(2,128)}, u32[]{:S(2)}) copy-start(s32[1,8,4,512,2]{3,4,2,1,0:T(2,128)} %param.13) | copy-start | bytes 393220
  21.3 22.5 %all-to-all-start.1 = ((bf16[16,4,2,8,512]{4,3,2,1,0:T(8,128)(2,1)}), bf16[16,4,2,8,512]{4,3,2,1,0:T(8,128)(2,1)S(1)}, u32[]{:S(2)}, u32[]{:S(2)}) async-start(bf16[16,4,2,8,512]{4,3,2,1,0:T(8,128)(2,1)} %broadcast_in_dim.43), calls=%async_computation.1 | async-start | bytes 2097152 | tf_op jit(solution)/shard_map/all_to_all | solution.py:149
  29.0 1.1 copy-start.8
  44.9 19.3 %all-to-all-start = ((bf16[16,4,2,8,512]{4,3,2,1,0:T(8,128)(2,1)}), bf16[16,4,2,8,512]{4,3,2,1,0:T(8,128)(2,1)S(1)}, u32[]{:S(2)}, u32[]{:S(2)}) async-start(bf16[16,4,2,8,512]{4,3,2,1,0:T(8,128)(2,1)} %broadcast_in_dim.42), calls=%async_computation | async-start | bytes 2097152 | tf_op jit(solution)/shard_map/all_to_all | solution.py:149
  51.1 15.3 %copy-start.2 = (bf16[4,2,16,8,512]{4,3,2,1,0:T(8,128)(2,1)}, bf16[4,2,16,8,512]{4,3,2,1,0:T(8,128)(2,1)S(1)}, u32[]{:S(2)}) copy-start(bf16[4,2,16,8,512]{4,3,2,1,0:T(8,128)(2,1)S(1)} %copy.57) | copy-start | bytes 3145732
  51.1 27.6 %collective-permute-start.2 = (bf16[4,256,512]{2,1,0:T(8,128)(2,1)S(1)}, bf16[4,256,512]{2,1,0:T(8,128)(2,1)}, u32[]{:S(2)}, u32[]{:S(2)}) collective-permute-start(bf16[4,256,512]{2,1,0:T(8,128)(2,1)S(1)} %bitcast.83), channel_id=1, source_target_pairs={{0,8},{8,0},{1,9},{9,1},{2,10},{10,2},{3,11},{11,3},{4,12},{12,4},... | collective-permute-start | bytes 3145736 | tf_op jit(solution)/shard_map/ppermute | solution.py:151
  64.4 27.5 %copy-start.1 = (bf16[4,2,16,8,512]{4,3,2,1,0:T(8,128)(2,1)}, bf16[4,2,16,8,512]{4,3,2,1,0:T(8,128)(2,1)S(1)}, u32[]{:S(2)}) copy-start(bf16[4,2,16,8,512]{4,3,2,1,0:T(8,128)(2,1)S(1)} %copy.56) | copy-start | bytes 3145732
  64.4 40.7 %collective-permute-start.1 = (bf16[4,256,512]{2,1,0:T(8,128)(2,1)S(1)}, bf16[4,256,512]{2,1,0:T(8,128)(2,1)S(1)}, u32[]{:S(2)}, u32[]{:S(2)}) collective-permute-start(bf16[4,256,512]{2,1,0:T(8,128)(2,1)S(1)} %bitcast.80), channel_id=1, source_target_pairs={{0,8},{8,0},{1,9},{9,1},{2,10},{10,2},{3,11},{11,3},{4,12},{12,4},... | collective-permute-start | bytes 3145736 | tf_op jit(solution)/shard_map/ppermute | solution.py:151
  105.1 1.0 copy-start.3
  119.2 5.5 %copy-start = (f32[384,768]{1,0:T(8,128)S(1)}, f32[384,768]{1,0:T(8,128)}, u32[]{:S(2)}) copy-start(f32[384,768]{1,0:T(8,128)} %get-tuple-element.29) | copy-start | bytes 3538948
  120.6 4.0 %collective-permute-start.3 = (bf16[384,768]{1,0:T(8,128)(2,1)S(1)}, bf16[384,768]{1,0:T(8,128)(2,1)S(1)}, u32[]{:S(2)}, u32[]{:S(2)}) collective-permute-start(bf16[384,768]{1,0:T(8,128)(2,1)S(1)} %convert_element_type.39), channel_id=1, source_target_pairs={{0,8},{8,0},{1,9},{9,1},{2,10},{10,2},{3,11},{11,3},{4,12},{12,4},... | collective-permute-start | bytes 1769480 | tf_op jit(solution)/shard_map/ppermute | solution.py:206
